TPU v7x, 256 devices: a whole 4x4x8 slice. The times are simulated.
256 devices in a mesh: wide: 64 (over z_lo, x, y), narrow: 4 (over z_hi, core).
Axes of the slice: x: 4, y: 4, z: 8 (z_hi: 2, z_lo: 4; z = z_hi * 4 + z_lo), core: 2. Of those that a mesh axis runs over, the one named last changes fastest.
Arguments:
- constraint_mats: bfloat16 [1024, 256, 256], P(('narrow', 'wide')), may hold values from -0.375 to 0.375
- primal_matrix: bfloat16 [256, 256], replicated, may hold values from -0.25 to 0.25
- inverse_dual_iterate: bfloat16 [256, 256], replicated, may hold values from -0.25 to 0.25
Outputs:
- schur: float32 [1024, 1024], P(('narrow', 'wide'))
All inputs are finite; a program needn't handle non-finite values.
Results may differ from a plain program's by a relative error of at most 0.0029.
Values may be sent and summed in bfloat16 or wider, within the bound.
A program may use at most 64 MiB of HBM per device.

v0:
```python
import jax
import jax.numpy as jnp
from jax import lax
from jax.sharding import PartitionSpec as P


def contract(u_rows, constraint_row_stack):
    return lax.dot_general(
        u_rows, constraint_row_stack, (((1,), (1,)), ((), ())), preferred_element_type=jnp.float32
    )


def body(constraint_mats, primal_matrix, inverse_dual_iterate):
    count = constraint_mats.shape[0]
    order = constraint_mats.shape[1]
    wide = lax.axis_size("wide")
    left_product = jnp.einsum(
        "ab,ibc->iac", primal_matrix, constraint_mats, preferred_element_type=jnp.float32
    ).astype(jnp.bfloat16)
    product_matrices = jnp.einsum(
        "lsx,xm->lsm", left_product, inverse_dual_iterate, preferred_element_type=jnp.float32
    ).astype(jnp.bfloat16)
    u_flat = product_matrices.reshape(count, order * order)
    a_flat = constraint_mats.reshape(count, order * order)
    both = jnp.stack([u_flat, a_flat])
    pieces = lax.all_to_all(both, "wide", split_axis=2, concat_axis=1, tiled=True)
    every = lax.all_gather(pieces, "narrow", axis=1, tiled=True)
    partial_value = 0.5 * (contract(pieces[0], every[1]) + contract(pieces[1], every[0]))
    rows = partial_value.shape[0] // wide
    blocks = partial_value.reshape(wide, rows, partial_value.shape[1])
    arrived = lax.all_to_all(blocks, "wide", split_axis=0, concat_axis=0, tiled=True)
    return jnp.sum(arrived, axis=0)


def solution(mesh):
    in_specs = (P(("narrow", "wide"), None, None), P(), P())
    out_specs = P(("narrow", "wide"), None)
    return jax.shard_map(body, mesh=mesh, in_specs=in_specs, out_specs=out_specs, check_vma=False)
```

profile of v0, /device:TPU:1, one launch (start us, length us, event | category | flops | bytes accessed | tf_op | source)
XLA Modules:
  0.0 422.6 jit_solution(4422344716620643686)
XLA Ops:
  6.5 0.0 copy-start
  6.5 0.0 all-gather.2.cloned.1.call-start
  6.5 1.5 stack_reshape.7
  8.0 0.0 copy-done
  8.0 1.8 convolution_convert_fusion
  9.9 0.4 stack_reshape.6
  10.3 0.7 pad_maximum_fusion
  11.0 51.0 %copy.18 = bf16[2,4,65536]{1,0,2:T(2,128)(2,1)} copy(bf16[2,4,65536]{2,1,0:T(4,128)(2,1)S(1)} %pad_maximum_fusion) | data formatting | bytes 2097152 | tf_op jit(solution)/shard_map/stack | solution.py:25
  62.0 61.1 %reshape.10 = bf16[64,2,4096]{2,1,0:T(2,128)(2,1)S(1)} reshape(bf16[65536,2,4]{2,1,0:T(2,128)(2,1)} %bitcast.29) | data formatting | bytes 2097152
  123.2 39.6 %all_to_all.23 = bf16[64,2,4096]{2,1,0:T(2,128)(2,1)S(1)} all-to-all(bf16[64,2,4096]{2,1,0:T(2,128)(2,1)S(1)} %reshape.10), channel_id=1, replica_groups=mesh['wide'=64,'narrow'=4] {'wide'}, dimensions={0} | all-to-all | bytes 2097152 | tf_op jit(solution)/shard_map/all_to_all | solution.py:26
  162.8 73.3 %reshape.11 = bf16[65536,2,4]{2,1,0:T(2,128)(2,1)} reshape(bf16[64,2,4096]{2,1,0:T(2,128)(2,1)S(1)} %all_to_all.23) | data formatting | bytes 2097152
  236.1 65.3 %copy.19 = bf16[2,4,64,1024]{3,1,2,0:T(4,128)(2,1)S(1)} copy(bf16[2,4,64,1024]{1,0,3,2:T(2,128)(2,1)} %bitcast.30) | data formatting | bytes 2097152 | tf_op jit(solution)/shard_map/all_to_all | solution.py:26
  301.4 2.1 copy.20
  303.5 0.0 all-gather.2.cloned.1.call-update
  303.5 0.4 fusion.9
  303.9 0.1 squeeze.12
  304.0 0.1 squeeze.14
  304.1 65.0 %all-gather.2.cloned.1.call-done = bf16[2,1024,1024]{2,0,1:T(2,128)(2,1)} async-done(((bf16[2,256,1024]{2,0,1:T(2,128)(2,1)}), bf16[2,1024,1024]{2,0,1:T(2,128)(2,1)}) %all-gather.2.cloned.1.call-update) | async-done | bytes 4194320 | tf_op jit(solution)/shard_map/all_gather | solution.py:27
  369.1 8.9 %fusion.8 = (bf16[1,1024,1024]{2,0,1:T(2,128)(2,1)S(1)}, bf16[1,1024,1024]{2,0,1:T(2,128)(2,1)S(1)}) fusion(bf16[2,1024,1024]{2,0,1:T(2,128)(2,1)} %all-gather.2.cloned.1.call-done), kind=kLoop, calls=%fused_computation.12 | loop fusion | bytes 8388608 | tf_op jit(solution)/shard_map/slice | solution.py:28
  378.0 0.9 fusion
  378.9 0.0 copy-start.1
  379.0 1.0 fusion.3
  379.9 0.3 reshape.7
  380.3 34.7 %all_to_all.24 = f32[64,4,1024]{2,1,0:T(4,128)S(1)} all-to-all(f32[64,4,1024]{2,1,0:T(4,128)S(1)} %reshape.7), channel_id=1, replica_groups=mesh['wide'=64,'narrow'=4] {'wide'}, dimensions={0} | all-to-all | bytes 2097152 | tf_op jit(solution)/shard_map/all_to_all | solution.py:31
  415.0 0.8 reduce_sum.9
  415.8 0.0 copy-done.1
Async XLA Ops:
  6.5 1.5 copy-start
  6.5 362.6 %all-gather.2.cloned.1.call-start = ((), (), s32[]{:S(2)}) async-start(), calls=%async_computation.2 | async-start | bytes 5242880 | tf_op jit(solution)/shard_map/all_gather | solution.py:27
  378.9 36.8 %copy-start.1 = (bf16[256,256]{1,0:T(8,128)(2,1)S(1)}, bf16[256,256]{1,0:T(8,128)(2,1)}, u32[]{:S(2)}) copy-start(bf16[256,256]{1,0:T(8,128)(2,1)} %param.5) | copy-start | bytes 393220
Sparse Core Ops, SparseCore 0:
  303.6 65.4 all-gather.1
where the time goes:
time: 424 us; the launch traced here: 423 us
  local copies, waits for them, and re-layouts  265 us (62%)
  blocking collectives  74.3 us (18%)
  waiting for transfers between devices  65 us (15%)
  between operations  13.5 us (3%)
    unnamed x6, local copies, waits for them, and re-layouts  134 us
    all_to_all x2, local copies, waits for them, and re-layouts, body(): lax.all_to_all(both, 'wide', split_axis=2, concat_axis=1, tiled=True)  67.4 us
    all_gather x1, waiting for transfers between devices, body(): every = lax.all_gather(pieces, 'narrow', axis=1, tiled=True)  65 us
    another operation x3, local copies, waits for them, and re-layouts, body(): both = jnp.stack([u_flat, a_flat])  52.9 us
    all_to_all x1, blocking collectives, body(): lax.all_to_all(both, 'wide', split_axis=2, concat_axis=1, tiled=True)  39.6 us
    all_to_all x1, blocking collectives, body(): lax.all_to_all(blocks, 'wide', split_axis=0, concat_axis=0, tiled=True)  34.7 us
    slice x1, local copies, waits for them, and re-layouts, body(): every[1]  8.88 us
  transfers between devices with their start and end apart: 1, of which 1 were waited for; matrix products, arithmetic and copies ran while one was open for 0% of the time, Pallas kernels for 0%

commit v1 on v0

--- a/solution.py
+++ b/solution.py
@@ -24,7 +24,9 @@
     a_flat = constraint_mats.reshape(count, order * order)
     both = jnp.stack([u_flat, a_flat])
     pieces = lax.all_to_all(both, "wide", split_axis=2, concat_axis=1, tiled=True)
-    every = lax.all_gather(pieces, "narrow", axis=1, tiled=True)
+    every = jnp.concatenate(
+        lax.all_to_all(jnp.stack([pieces] * lax.axis_size("narrow")), "narrow", 0, 0), axis=1
+    )
     partial_value = 0.5 * (contract(pieces[0], every[1]) + contract(pieces[1], every[0]))
     rows = partial_value.shape[0] // wide
     blocks = partial_value.reshape(wide, rows, partial_value.shape[1])

time: 424 us -> 442 us (1.042)
  blocking collectives: 74.3 us -> 89.6 us
  between operations: 13.5 us -> 0.12 us
  waiting for transfers between devices: 65 us -> 76.8 us
  starting transfers between devices: 0.01 us -> 8.39 us
  local copies, waits for them, and re-layouts: 265 us -> 260 us
    all_to_all x0 -> x1, waiting for transfers between devices: none -> 76.8 us  [body(): lax.all_to_all(jnp.stack([pieces] * lax.axis_size('narrow')), 'narrow', 0...]
    all_gather x1 -> x0, waiting for transfers between devices: 65 us -> none  [body(): every = lax.all_gather(pieces, 'narrow', axis=1, tiled=True)]
    all_to_all x1, blocking collectives: 34.7 us -> 50 us  [body(): lax.all_to_all(blocks, 'wide', split_axis=0, concat_axis=0, tiled=True)]
    all_to_all x0 -> x1, starting transfers between devices: none -> 8.39 us  [body(): lax.all_to_all(jnp.stack([pieces] * lax.axis_size('narrow')), 'narrow', 0...]
    slice x2, local copies, waits for them, and re-layouts: 9.25 us -> 3.05 us  [the longest x1 2.69 us: body(): every[0]]
where the time goes in v1:
time: 442 us; the launch traced here: 440 us
  local copies, waits for them, and re-layouts  260 us (59%)
  blocking collectives  89.6 us (20%)
  waiting for transfers between devices  76.8 us (17%)
  starting transfers between devices  8.39 us (2%)
    unnamed x6, local copies, waits for them, and re-layouts  134 us
    all_to_all x1, waiting for transfers between devices, body(): lax.all_to_all(jnp.stack([pieces] * lax.axis_size('narrow')), 'narrow', 0...  76.8 us
    all_to_all x2, local copies, waits for them, and re-layouts, body(): lax.all_to_all(both, 'wide', split_axis=2, concat_axis=1, tiled=True)  66.4 us
    another operation x3, local copies, waits for them, and re-layouts, body(): both = jnp.stack([u_flat, a_flat])  52.8 us
    all_to_all x1, blocking collectives, body(): lax.all_to_all(blocks, 'wide', split_axis=0, concat_axis=0, tiled=True)  50 us
    all_to_all x1, blocking collectives, body(): lax.all_to_all(both, 'wide', split_axis=2, concat_axis=1, tiled=True)  39.6 us
  transfers between devices with their start and end apart: 1, of which 1 were waited for; matrix products, arithmetic and copies ran while one was open for 0% of the time, Pallas kernels for 0%

profile of v1, /device:TPU:1, one launch (start us, length us, event | category | flops | bytes accessed | tf_op | source)
XLA Modules:
  0.0 439.9 jit_solution(38121477208475116)
XLA Ops:
  0.0 0.0 copy-start
  0.0 1.5 stack_reshape.7
  1.5 0.0 copy-done
  1.5 1.8 convolution_convert_fusion
  3.3 0.4 stack_reshape.6
  3.7 0.7 pad_maximum_fusion
  4.5 50.9 %copy.15 = bf16[2,4,65536]{1,0,2:T(2,128)(2,1)} copy(bf16[2,4,65536]{2,1,0:T(4,128)(2,1)S(1)} %pad_maximum_fusion) | data formatting | bytes 2097152 | tf_op jit(solution)/shard_map/stack | solution.py:25
  55.4 61.1 %reshape.22 = bf16[64,2,4096]{2,1,0:T(2,128)(2,1)S(1)} reshape(bf16[65536,2,4]{2,1,0:T(2,128)(2,1)} %bitcast.24) | data formatting | bytes 2097152
  116.5 39.6 %all_to_all.25 = bf16[64,2,4096]{2,1,0:T(2,128)(2,1)S(1)} all-to-all(bf16[64,2,4096]{2,1,0:T(2,128)(2,1)S(1)} %reshape.22), channel_id=1, replica_groups=mesh['wide'=64,'narrow'=4] {'wide'}, dimensions={0} | all-to-all | bytes 2097152 | tf_op jit(solution)/shard_map/all_to_all | solution.py:26
  156.1 73.3 %reshape.23 = bf16[65536,2,4]{2,1,0:T(2,128)(2,1)} reshape(bf16[64,2,4096]{2,1,0:T(2,128)(2,1)S(1)} %all_to_all.25) | data formatting | bytes 2097152
  229.4 65.3 %copy.16 = bf16[2,4,64,1024]{3,1,2,0:T(4,128)(2,1)S(1)} copy(bf16[2,4,64,1024]{1,0,3,2:T(2,128)(2,1)} %bitcast.25) | data formatting | bytes 2097152 | tf_op jit(solution)/shard_map/all_to_all | solution.py:26
  294.8 1.1 copy.17
  295.8 0.3 copy.18
  296.1 2.5 stack.14
  298.6 8.4 %all-to-all-start.1 = ((bf16[4,2,256,1024]{3,2,1,0:T(8,128)(2,1)}), bf16[4,2,256,1024]{3,2,1,0:T(8,128)(2,1)}, u32[]{:S(2)}, u32[]{:S(2)}) async-start(bf16[4,2,256,1024]{3,2,1,0:T(8,128)(2,1)} %stack.14), calls=%async_computation.1 | async-start | bytes 8388608 | tf_op jit(solution)/shard_map/all_to_all | solution.py:28
  307.0 0.4 fusion.6
  307.4 0.1 squeeze.14
  307.5 0.1 squeeze.12
  307.6 76.8 %all-to-all-done.1 = bf16[4,2,256,1024]{3,2,1,0:T(8,128)(2,1)} async-done(((bf16[4,2,256,1024]{3,2,1,0:T(8,128)(2,1)}), bf16[4,2,256,1024]{3,2,1,0:T(8,128)(2,1)}, u32[]{:S(2)}, u32[]{:S(2)}) %all-to-all-start.1) | async-done | bytes 4194336 | tf_op jit(solution)/shard_map/all_to_all | solution.py:28
  384.5 2.7 fusion.5
  387.2 0.8 fusion.7
  388.0 0.8 fusion
  388.8 0.0 copy-start.1
  388.8 0.3 reshape.19
  389.1 50.0 %all_to_all.26 = f32[64,4,1024]{2,1,0:T(4,128)S(1)} all-to-all(f32[64,4,1024]{2,1,0:T(4,128)S(1)} %reshape.19), channel_id=1, replica_groups=mesh['wide'=64,'narrow'=4] {'wide'}, dimensions={0} | all-to-all | bytes 2097152 | tf_op jit(solution)/shard_map/all_to_all | solution.py:33
  439.1 0.8 reduce_sum.9
  439.9 0.0 copy-done.1
Async XLA Ops:
  0.0 1.5 copy-start
  298.6 85.8 %all-to-all-start.1 = ((bf16[4,2,256,1024]{3,2,1,0:T(8,128)(2,1)}), bf16[4,2,256,1024]{3,2,1,0:T(8,128)(2,1)}, u32[]{:S(2)}, u32[]{:S(2)}) async-start(bf16[4,2,256,1024]{3,2,1,0:T(8,128)(2,1)} %stack.14), calls=%async_computation.1 | async-start | bytes 8388608 | tf_op jit(solution)/shard_map/all_to_all | solution.py:28
  388.8 51.2 %copy-start.1 = (bf16[256,256]{1,0:T(8,128)(2,1)S(1)}, bf16[256,256]{1,0:T(8,128)(2,1)}, u32[]{:S(2)}) copy-start(bf16[256,256]{1,0:T(8,128)(2,1)} %param.5) | copy-start | bytes 393220

commit v2 on v0

--- a/solution.py
+++ b/solution.py
@@ -23,7 +23,10 @@
     u_flat = product_matrices.reshape(count, order * order)
     a_flat = constraint_mats.reshape(count, order * order)
     both = jnp.stack([u_flat, a_flat])
-    pieces = lax.all_to_all(both, "wide", split_axis=2, concat_axis=1, tiled=True)
+    pieces = jnp.concatenate(
+        lax.all_to_all(jnp.stack(jnp.split(both, lax.axis_size("wide"), axis=2)), "wide", 0, 0),
+        axis=1,
+    )
     every = lax.all_gather(pieces, "narrow", axis=1, tiled=True)
     partial_value = 0.5 * (contract(pieces[0], every[1]) + contract(pieces[1], every[0]))
     rows = partial_value.shape[0] // wide

time: 424 us -> 173 us (0.41)
  local copies, waits for them, and re-layouts: 265 us -> 15 us
    unnamed x6 -> x66, local copies, waits for them, and re-layouts: 134 us -> 1.14 us
    all_to_all x2 -> x0, local copies, waits for them, and re-layouts: 67.4 us -> none  [body(): lax.all_to_all(both, 'wide', split_axis=2, concat_axis=1, tiled=True)]
    another operation x3, local copies, waits for them, and re-layouts: 52.9 us -> 2.08 us  [body(): both = jnp.stack([u_flat, a_flat])]
where the time goes in v2:
time: 173 us
  blocking collectives  74.3 us (43%)
  waiting for transfers between devices  65 us (38%)
  local copies, waits for them, and re-layouts  15 us (9%)
  between operations  13.8 us (8%)
  matrix products  3.74 us (2%)
    all_gather x1, waiting for transfers between devices, body(): every = lax.all_gather(pieces, 'narrow', axis=1, tiled=True)  65 us
    all_to_all x1, blocking collectives, body(): lax.all_to_all(jnp.stack(jnp.split(both, lax.axis_size('wide'), axis=2)),...  39.6 us
    all_to_all x1, blocking collectives, body(): lax.all_to_all(blocks, 'wide', split_axis=0, concat_axis=0, tiled=True)  34.7 us
    slice x1, local copies, waits for them, and re-layouts, body(): every[1]  8.81 us
  transfers between devices with their start and end apart: 1, of which 1 were waited for; matrix products, arithmetic and copies ran while one was open for 0% of the time, Pallas kernels for 0%

profile of v2, /device:TPU:1, one launch (start us, length us, event | category | flops | bytes accessed | tf_op | source)
XLA Modules:
  0.0 172.7 jit_solution(320172197890776471)
XLA Ops:
  6.5 0.0 copy-start
  6.5 0.0 all-gather.2.cloned.1.call-start
  6.5 1.5 stack_reshape.7
  8.0 0.0 copy-done
  8.0 1.8 %convolution_convert_fusion = bf16[4,256,256]{2,1,0:T(8,128)(2,1)S(1)} fusion(bf16[4,256,256]{2,1,0:T(8,128)(2,1)} %param.3, bf16[256,256]{1,0:T(8,128)(2,1)S(1)} %copy-done, bf16[256,256]{1,0:T(8,128)(2,1)} %param.4), kind=kOutput, calls=%fused_computation.6 | convolution fusion | flops 268959744 | bytes 1310720 | tf_op jit(solution)/shard_map/lsx,xm->lsm/dot_general | solution.py:20
  9.9 0.4 stack_reshape.6
  10.3 0.2 constant_dynamic-update-slice_fusion.1
  10.5 0.2 constant_dynamic-update-slice_fusion
  12.0 39.6 %all_to_all.10 = bf16[64,2,4,1024]{3,2,1,0:T(4,128)(2,1)S(1)} all-to-all(bf16[64,2,4,1024]{3,2,1,0:T(4,128)(2,1)S(1)} %constant_dynamic-update-slice_fusion.2), channel_id=1, replica_groups=mesh['wide'=64,'narrow'=4] {'wide'}, dimensions={0} | all-to-all | bytes 2097152 | tf_op jit(solution)/shard_map/all_to_all | solution.py:27
  51.6 2.1 %copy.74 = bf16[2,64,4,1024]{3,0,2,1:T(2,128)(2,1)} copy(bf16[2,64,4,1024]{3,2,0,1:T(4,128)(2,1)S(1)} %bitcast.286) | data formatting | bytes 2097152 | tf_op jit(solution)/shard_map/reshape | solution.py:26
  53.6 0.0 all-gather.2.cloned.1.call-update
  53.7 0.4 fusion.9
  54.0 0.1 squeeze.12
  54.2 0.1 squeeze.14
  54.3 65.0 %all-gather.2.cloned.1.call-done = bf16[2,1024,1024]{2,0,1:T(2,128)(2,1)} async-done(((bf16[2,256,1024]{2,0,1:T(2,128)(2,1)}), bf16[2,1024,1024]{2,0,1:T(2,128)(2,1)}) %all-gather.2.cloned.1.call-update) | async-done | bytes 4194320 | tf_op jit(solution)/shard_map/all_gather | solution.py:30
  119.3 8.8 %fusion.8 = (bf16[1,1024,1024]{2,0,1:T(2,128)(2,1)S(1)}, bf16[1,1024,1024]{2,0,1:T(2,128)(2,1)S(1)}) fusion(bf16[2,1024,1024]{2,0,1:T(2,128)(2,1)} %all-gather.2.cloned.1.call-done), kind=kLoop, calls=%fused_computation.141 | loop fusion | bytes 8388608 | tf_op jit(solution)/shard_map/slice | solution.py:31
  128.1 0.9 fusion
  129.1 1.0 fusion.3
  130.0 0.3 reshape.15
  130.4 34.7 %all_to_all.11 = f32[64,4,1024]{2,1,0:T(4,128)S(1)} all-to-all(f32[64,4,1024]{2,1,0:T(4,128)S(1)} %reshape.15), channel_id=1, replica_groups=mesh['wide'=64,'narrow'=4] {'wide'}, dimensions={0} | all-to-all | bytes 2097152 | tf_op jit(solution)/shard_map/all_to_all | solution.py:34
  165.1 0.8 reduce_sum.9
  (64 shorter events, 1.0 us)
Async XLA Ops:
  6.5 1.5 copy-start
  6.5 112.8 %all-gather.2.cloned.1.call-start = ((), (), s32[]{:S(2)}) async-start(), calls=%async_computation.2 | async-start | bytes 5242880 | tf_op jit(solution)/shard_map/all_gather | solution.py:30
Sparse Core Ops, SparseCore 0:
  53.8 65.4 all-gather.1
